TPU v7x, 32 devices: a whole 2x2x4 slice. The times are simulated.
32 devices in a mesh: vit: 2 (over y), seq: 4 (over z), tensor: 4 (over x, core).
Axes of the slice: x: 2, y: 2, z: 4, core: 2. Of those that a mesh axis runs over, the one named last changes fastest.
Arguments:
- merged: bfloat16 [256, 8192], P(('vit', 'seq'), 'tensor'), may hold values from -6 to 6
- positions: int32 [256], P(('vit', 'seq')), may hold values from 0 to 65535, as said below
- picked: int32 [256], P(('vit', 'seq')), may hold values from 0 to 1, as said below
- router_score: float32 [256], P(('vit', 'seq')), may hold values from -8 to 8
- up_weight: bfloat16 [8192, 16384], P('tensor', ('vit', 'seq')), may hold values from -0.0625 to 0.0625
- down_weight: bfloat16 [16384, 8192], P(('vit', 'seq'), 'tensor'), may hold values from -0.046875 to 0.046875
- mixed_grad: bfloat16 [64, 8192], P(('vit', 'seq'), 'tensor'), may hold values from -6 to 6
Outputs:
- mixed: bfloat16 [64, 8192], P(('vit', 'seq'), 'tensor')
- token_grad: bfloat16 [256, 8192], P(('vit', 'seq'), 'tensor')
- up_grad: float32 [8192, 16384], P('tensor', ('vit', 'seq'))
- down_grad: float32 [16384, 8192], P(('vit', 'seq'), 'tensor')
Inputs may be any that keep to these rules, and one draw needn't show every extreme that they name: Among the picked tokens of one aligned block of 32 tokens, at most 2 have the same positions // 16384, and in every block some value of positions // 16384 is shared by exactly 2 picked tokens. `picked`: exactly 8 ones in every aligned block of 32 tokens.
All inputs are finite; a program needn't handle non-finite values.
Results may differ from a plain program's by a relative error of at most 0.0056.
Values may be sent and summed in bfloat16 or wider, within the bound.
No kernel may reach another device: no remote copies, remote signals or barrier semaphores. Data moves between devices by JAX's collectives and lax.ppermute only.
A program may use at most 128 MiB of HBM per device.

v0:
```python
import functools

import jax
import jax.numpy as jnp
from jax import lax
from jax.experimental import pallas as pl
from jax.experimental.pallas import tpu as pltpu
from jax.sharding import PartitionSpec as P


CAP = 2
SPAN = 16384
LANES = 128
MIB = 1 << 20
PARTS = 4

F32 = jnp.float32
BF16 = jnp.bfloat16
VMEM = pltpu.MemorySpace.VMEM
IN_VMEM = pl.BlockSpec(memory_space=VMEM)
IN_HBM = pl.BlockSpec(memory_space=pltpu.MemorySpace.HBM)
IN_PLACE = pl.BlockSpec(memory_space=pl.ANY)
AS_IS = (((1,), (0,)), ((), ()))
TURNED = (((1,), (1,)), ((), ()))


def in_hbm(array):
    return pltpu.with_memory_space_constraint(array, pltpu.MemorySpace.HBM)


def params(mib):
    return pltpu.CompilerParams(vmem_limit_bytes=mib * MIB)


def held(shape, dtype):
    return jax.ShapeDtypeStruct(shape, dtype)


def cost(flops, moved):
    return pl.CostEstimate(flops=int(flops), bytes_accessed=int(moved), transcendentals=0)


def swap(value, axis, bit):
    size = lax.axis_size(axis)
    return lax.ppermute(value, axis, [(i, i ^ bit) for i in range(size)])


def other_half(size):
    return pl.multiple_of((1 - lax.rem(lax.axis_index("tensor"), 2)) * size, size)


def own_half(size):
    return pl.multiple_of(lax.rem(lax.axis_index("tensor"), 2) * size, size)


def load_kernel(wheres, *refs):
    source, outs, sems = refs[0], refs[1:-1], refs[-1]
    copies = []
    for where, out in zip(wheres, outs):
        rows, columns = out.shape
        at = own_half if where == "own" else other_half
        row = at(rows) if rows < source.shape[0] else 0
        column = at(columns) if columns < source.shape[1] else 0
        each = rows // PARTS
        for i in range(PARTS):
            part = source.at[pl.ds(row + i * each, each), pl.ds(column, columns)]
            copies.append(
                pltpu.make_async_copy(part, out.at[pl.ds(i * each, each)], sems.at[len(copies)])
            )
    for copy in copies:
        copy.start()
    for copy in copies:
        copy.wait()


def load(weights, wheres, rows, columns):
    return pl.pallas_call(
        functools.partial(load_kernel, wheres),
        out_shape=[pltpu.VMEM((rows, columns), weights.dtype)] * len(wheres),
        in_specs=[IN_PLACE],
        out_specs=[IN_VMEM] * len(wheres),
        scratch_shapes=[pltpu.SemaphoreType.DMA((PARTS * len(wheres),))],
        compiler_params=params(2),
        cost_estimate=cost(0, 2 * len(wheres) * rows * columns),
        name="load",
    )(in_hbm(weights))


def gather_pieces(piece, up, down):
    seqs, vits = lax.axis_size("seq"), lax.axis_size("vit")
    deep, hidden = up.shape
    piece, up = lax.optimization_barrier((piece, up))
    along = [piece] + [swap(piece, "seq", k) for k in range(1, seqs)]
    near = along[: seqs // 2]
    near, up, down = lax.optimization_barrier((near, up, down))
    (up,) = load(up, ("other",), deep, hidden // 2)
    (sent,) = load(down, ("other",), hidden // 2, deep)
    far, up, sent, down = lax.optimization_barrier((along[seqs // 2 :], up, sent, down))
    along = near + far
    out = list(along)
    for v in range(1, vits):
        out += [swap(p, "vit", v) for p in along]
    (kept,) = load(down, ("own",), hidden // 2, deep)
    return (out, *lax.optimization_barrier((up, sent, kept)))


def sum_over_vit(blocks):
    v = lax.axis_index("vit")
    total = lax.dynamic_index_in_dim(blocks, v, 0, False).astype(F32)
    for k in range(1, lax.axis_size("vit")):
        total = total + swap(lax.dynamic_index_in_dim(blocks, v ^ k, 0, False), "vit", k).astype(F32)
    return total.astype(BF16)


def pieces_over_seq(blocks):
    s = lax.axis_index("seq")
    out = [lax.dynamic_index_in_dim(blocks, s, 0, False)]
    for k in range(1, lax.axis_size("seq")):
        out.append(swap(lax.dynamic_index_in_dim(blocks, s ^ k, 0, False), "seq", k))
    return out


def route_kernel(seqs, *refs):
    sources, (piece, place), copied, sems = refs[:5], refs[5:7], refs[7:12], refs[12]
    copies = [pltpu.make_async_copy(sources[i], copied[i], sems.at[i]) for i in range(5)]
    for copy in copies:
        copy.start()
    for copy in copies[:3]:
        copy.wait()
    pos, picked, score, merged, cotangent = copied
    local, tokens = place.shape
    width = merged.shape[1]
    taken = picked[...] == 1
    target = lax.shift_right_logical(pos[...], SPAN.bit_length() - 1)
    owner = lax.broadcasted_iota(jnp.int32, (seqs, tokens), 0)
    onehot = jnp.where((owner == target) & taken, 1.0, 0.0)
    before = lax.broadcasted_iota(jnp.int32, (tokens, tokens), 0) < lax.broadcasted_iota(
        jnp.int32, (tokens, tokens), 1
    )
    before = jnp.where(before, 1.0, 0.0).astype(BF16)
    earlier = jnp.dot(onehot.astype(BF16), before, preferred_element_type=F32)
    rank = jnp.sum(earlier * onehot, axis=0, keepdims=True)
    slot = target.astype(F32) * CAP + rank
    wanted = lax.broadcasted_iota(jnp.int32, (local, tokens), 0).astype(F32)
    chosen = jnp.where((wanted == slot) & taken, 1.0, 0.0)
    place[...] = chosen.astype(BF16)
    gate = jax.nn.sigmoid(score[...]).astype(BF16).astype(F32)
    gates = jnp.sum(chosen * gate, axis=1, keepdims=True)
    piece[0:local, width : width + LANES] = jnp.broadcast_to(gates, (local, LANES)).astype(BF16)
    for copy in copies[3:]:
        copy.wait()
    rows = jnp.dot(chosen.astype(BF16), merged[...], preferred_element_type=F32)
    piece[0:local, 0:width] = rows.astype(BF16)
    piece[local : 2 * local, 0:width] = cotangent[...]
    piece[local : 2 * local, width : width + LANES] = jnp.zeros((local, LANES), BF16)


def route(positions, picked, score, merged, cotangent):
    local, width = cotangent.shape
    tokens = merged.shape[0]
    arrays = (positions[None], picked[None], score[None], merged, cotangent)
    return pl.pallas_call(
        functools.partial(route_kernel, lax.axis_size("seq")),
        out_shape=[pltpu.VMEM((2 * local, width + LANES), BF16), held((local, tokens), BF16)],
        in_specs=[IN_HBM] * 5,
        out_specs=[IN_VMEM] * 2,
        scratch_shapes=[pltpu.VMEM(a.shape, a.dtype) for a in arrays] + [pltpu.SemaphoreType.DMA((5,))],
        compiler_params=params(4),
        name="route",
    )(*[in_hbm(a) for a in arrays])


def product(left, weights, turned, start, size, out):
    tile = min(512, size)

    def step(j, carry):
        src = pl.ds(pl.multiple_of(start + j * tile, tile), tile)
        part = weights[src, :] if turned else weights[:, src]
        term = lax.dot_general(left, part, TURNED if turned else AS_IS, preferred_element_type=F32)
        out[:, pl.ds(pl.multiple_of(j * tile, tile), tile)] = term.astype(out.dtype)
        return carry

    lax.fori_loop(0, size // tile, step, 0)


def first_kernel(seqs, count, *refs):
    pieces, up_sent, up = refs[:count], refs[count], refs[count + 1]
    rows, scaled, mine, sent, kept, together, chunks, sems = refs[count + 2 :]
    slots, width = rows.shape
    half = sent.shape[1]
    coming = Stream(up, False, 0, own_half(half), chunks, sems)
    local = slots // count
    v, s = lax.axis_index("vit"), lax.axis_index("seq")
    me = v * seqs + s
    for k in range(count):
        together[2 * local * k : 2 * local * (k + 1), :] = pieces[k][...]
    total = 2 * slots
    c = lax.broadcasted_iota(jnp.int32, (1, total), 1)
    dev = (c // (2 * local)) ^ me
    j = c % (2 * local)
    slot_row = ((dev // seqs) * seqs + j // CAP) * local + (dev % seqs) * CAP + j % CAP
    slot = jnp.where(j < local, slot_row, slots + dev * local + j - local)
    wanted = lax.broadcasted_iota(jnp.int32, (total, total), 0)
    order = jnp.where(wanted == slot, 1.0, 0.0).astype(BF16)
    data = together[...]
    got = jnp.dot(order, data, preferred_element_type=F32)
    i = lax.broadcasted_iota(jnp.int32, (2 * local, total), 0)
    own = slots + (v * seqs + (i - local) // CAP) * local + s * CAP + i % CAP
    own = jnp.where(i < local, me * local + i, own)
    pick = jnp.where(own == slot, 1.0, 0.0).astype(BF16)
    mine[...] = jnp.dot(pick, data, preferred_element_type=F32).astype(BF16)
    rows[...] = got[:slots, :width].astype(BF16)
    scaled[...] = (got[:slots, width : width + 1] * got[slots:, :width]).astype(BF16)
    product(rows[...], up_sent, False, 0, half, sent)

    def store(where, value):
        kept[:, where] = value

    coming.finish(rows, store)


def first(pieces, up_sent, up):
    count = len(pieces)
    two, wide = pieces[0].shape
    slots, width = count * two // 2, wide - LANES
    half = up.shape[1] // 2
    return pl.pallas_call(
        functools.partial(first_kernel, lax.axis_size("seq"), count),
        out_shape=[
            held((slots, width), BF16),
            held((slots, width), BF16),
            held((two, wide), BF16),
            held((slots, half), BF16),
            held((slots, half), F32),
        ],
        in_specs=[IN_VMEM] * (count + 1) + [IN_PLACE],
        out_specs=[IN_VMEM] * 5,
        scratch_shapes=[pltpu.VMEM((2 * slots, wide), BF16), *stream_scratch(up, False, width, half)],
        compiler_params=params(6 + (30 * slots * wide + 2 * width * half) // MIB),
        cost_estimate=cost(2 * slots * up.size, 2 * up.size),
        name="first",
    )(*pieces, up_sent, in_hbm(up))


def act_grad_kernel(scaled, down, out, *again):
    if again:
        copy = pltpu.make_async_copy(down, again[0], again[1])
        copy.start()
    product(scaled[...], down, True, 0, out.shape[1], out)
    if again:
        copy.wait()


def act_grad_half(scaled, down, dtype, again=False):
    slots, half = scaled.shape[0], down.shape[0]
    return pl.pallas_call(
        act_grad_kernel,
        out_shape=[held((slots, half), dtype)] + [pltpu.VMEM(down.shape, down.dtype)] * again,
        in_specs=[IN_VMEM] * 2,
        out_specs=[IN_VMEM] * (1 + again),
        scratch_shapes=[pltpu.SemaphoreType.DMA] * again,
        compiler_params=params(6 + 12 * slots * half // MIB),
        cost_estimate=cost(2 * slots * down.size, 2 * down.size),
        name="act_grad",
    )(scaled, down)


class Stream:
    def __init__(self, weights, turned, row, column, chunks, sems):
        self.turned, self.chunks, self.sems = turned, chunks, sems
        count, tall, wide = chunks.shape
        self.copies = []
        for i in range(count):
            begin = (row + i * tall, column) if turned else (row, column + i * wide)
            source = weights.at[pl.ds(begin[0], tall), pl.ds(begin[1], wide)]
            self.copies.append(pltpu.make_async_copy(source, chunks.at[i], sems.at[i]))
        for copy in self.copies:
            copy.start()

    def finish(self, left, store):
        value = left[...]
        _, tall, wide = self.chunks.shape
        tile = tall if self.turned else wide
        for i, copy in enumerate(self.copies):
            copy.wait()
            store(
                slice(i * tile, (i + 1) * tile),
                lax.dot_general(
                    value,
                    self.chunks[i],
                    TURNED if self.turned else AS_IS,
                    preferred_element_type=F32,
                ),
            )


def stream_scratch(weights, turned, deep, across):
    tile = min(512, across)
    count = across // tile
    shape = (count, tile, deep) if turned else (count, deep, tile)
    return [pltpu.VMEM(shape, weights.dtype), pltpu.SemaphoreType.DMA((count,))]


def y_kernel(own, other, down_own, down_other, out):
    y = jnp.dot(own[...], down_own[...], preferred_element_type=F32)
    y = y + jnp.dot(other[...], down_other[...], preferred_element_type=F32)
    out[...] = y.astype(out.dtype)


def y_terms(own, other, down_own, down_other):
    slots, half = own.shape
    width = down_own.shape[1]
    return pl.pallas_call(
        y_kernel,
        out_shape=held((slots, width), BF16),
        in_specs=[IN_VMEM] * 4,
        out_specs=IN_VMEM,
        compiler_params=params(6 + 24 * slots * width // MIB),
        cost_estimate=cost(4 * slots * half * width, 4 * half * width),
        name="y",
    )(own, other, down_own, down_other)


def row_kernel(own, up, out, chunks, sems):
    coming = Stream(up, True, 0, own_half(own.shape[1]), chunks, sems)

    def store(where, value):
        out[:, where] = value

    coming.finish(own, store)


def row_part(own, up):
    slots, half = own.shape
    width = up.shape[0]
    return pl.pallas_call(
        row_kernel,
        out_shape=held((slots, width), F32),
        in_specs=[IN_VMEM, IN_PLACE],
        out_specs=IN_VMEM,
        scratch_shapes=stream_scratch(up, True, half, width),
        compiler_params=params(6 + (up.size + 24 * slots * width) // MIB),
        cost_estimate=cost(slots * up.size, up.size),
        name="row_part",
    )(own, in_hbm(up))


def terms_kernel(seqs, local, other, before, y, up, terms, chunks, sems, term):
    slots, half = other.shape
    coming = Stream(up, True, 0, other_half(half), chunks, sems)
    r = lax.broadcasted_iota(jnp.int32, (2 * slots, 1), 0)
    d, j = r // (2 * local), r % (2 * local)
    src = ((d // seqs) * seqs + (j - local) // CAP) * local + (d % seqs) * CAP + j % CAP
    src = jnp.where(j < local, d * local + j, slots + src)
    order = jnp.where(src == lax.broadcasted_iota(jnp.int32, (2 * slots, 2 * slots), 1), 1.0, 0.0)
    order = order.astype(BF16)
    term[:slots, :] = y[...]

    def store(where, value):
        term[slots:, where] = (value + before[:, where]).astype(BF16)
        both = jnp.dot(order, term[:, where], preferred_element_type=F32)
        terms[:, where] = both.astype(BF16)

    coming.finish(other, store)


def all_terms(other, before, y, up, local):
    slots, half = other.shape
    width = up.shape[0]
    return pl.pallas_call(
        functools.partial(terms_kernel, lax.axis_size("seq"), local),
        out_shape=held((2 * slots, width), BF16),
        in_specs=[IN_VMEM] * 3 + [IN_PLACE],
        out_specs=IN_VMEM,
        scratch_shapes=[
            *stream_scratch(up, True, half, width),
            pltpu.VMEM((2 * slots, width), BF16),
        ],
        compiler_params=params(6 + (up.size + 32 * slots * width) // MIB),
        cost_estimate=cost(slots * up.size, up.size),
        name="all_terms",
    )(other, before, y, in_hbm(up))


def weight_grads_kernel(ahead, begin, *refs):
    if ahead:
        act, act_other, scaled, rows, own, other, down_grad, up_grad, buf, sems, whole = refs
    else:
        rows, own, other, _, up_grad, buf, sems, whole = refs
    half = own.shape[1]
    flights, tile = buf.shape[0], buf.shape[1]
    whole[:, pl.ds(own_half(half), half)] = own[...]
    whole[:, pl.ds(other_half(half), half)] = other[...]
    jobs = []
    if ahead:
        each = half // tile
        for i in range(2 * each):
            left, start = (act, own_half(half)) if i < each else (act_other, other_half(half))
            jobs.append((left, (i % each) * tile, scaled, down_grad, start + (i % each) * tile))
    for i in range(*begin):
        jobs.append((rows, i * tile, whole, up_grad, i * tile))

    def copy(i):
        slot, width = i % flights, jobs[i][3].shape[1]
        return pltpu.make_async_copy(
            buf.at[slot, :, pl.ds(0, width)], jobs[i][3].at[pl.ds(jobs[i][4], tile)], sems.at[slot]
        )

    for i, (left, at, right, out, unused_start) in enumerate(jobs):
        if i >= flights:
            copy(i - flights).wait()
        buf[i % flights, :, : out.shape[1]] = lax.dot_general(
            left[:, at : at + tile], right[...], (((0,), (0,)), ((), ())), preferred_element_type=F32
        )
        copy(i).start()
    for i in range(max(0, len(jobs) - flights), len(jobs)):
        copy(i).wait()


def weight_grads(tile, begin, operands, shapes, ahead, before=()):
    flights, widest = 4, max(shape[1] for shape in shapes)
    slots, hidden = operands[-1].shape[0], 2 * operands[-1].shape[1]
    written = sum(shape[0] * shape[1] for shape in shapes)
    return pl.pallas_call(
        functools.partial(weight_grads_kernel, ahead, begin),
        out_shape=[held(shape, F32) for shape in shapes],
        in_specs=[IN_VMEM] * len(operands) + [IN_PLACE] * len(before),
        out_specs=[IN_PLACE] * len(shapes),
        scratch_shapes=[
            pltpu.VMEM((flights, tile, widest), F32),
            pltpu.SemaphoreType.DMA((flights,)),
            pltpu.VMEM((slots, hidden), BF16),
        ],
        input_output_aliases={len(operands): 0} if before else {},
        compiler_params=params(26),
        cost_estimate=cost(2 * slots * written, 3 * written),
        name="weight_grads",
    )(*operands, *before)


def final_kernel(count, *refs):
    pieces, mine, place, mixed, token_grad = refs[:count], *refs[count:]
    local, width = mixed.shape
    sums = pieces[0][...].astype(F32)
    for piece in pieces[1:]:
        sums = sums + piece[...].astype(F32)
    gates = mine[:local, width : width + 1].astype(F32)
    mixed[...] = (mine[:local, :width].astype(F32) + gates * sums[:local]).astype(BF16)
    slot_grad = (mine[local:, :width].astype(F32) + sums[local:]).astype(BF16)
    token_grad[...] = lax.dot_general(
        place[...], slot_grad, (((0,), (0,)), ((), ())), preferred_element_type=F32
    ).astype(BF16)


def final(pieces, mine, place):
    _, width = pieces[0].shape
    local, tokens = place.shape
    return pl.pallas_call(
        functools.partial(final_kernel, len(pieces)),
        out_shape=[held((local, width), BF16), held((tokens, width), BF16)],
        in_specs=[IN_VMEM] * (len(pieces) + 2),
        out_specs=[IN_VMEM] * 2,
        compiler_params=params(6),
        name="final",
    )(*pieces, mine, place)


def over_chips(total, bit=2):
    while bit < lax.axis_size("tensor"):
        total = total + swap(total.astype(BF16), "tensor", bit).astype(F32)
        bit *= 2
    return total


def per_device(merged, positions, picked, router_score, up_weight, down_weight, mixed_grad):
    local, width = mixed_grad.shape
    seqs, vits = lax.axis_size("seq"), lax.axis_size("vit")
    hidden = up_weight.shape[1]
    piece, place = route(positions, picked, router_score, merged, mixed_grad)
    pieces, up_sent, down_sent, down_kept = gather_pieces(piece, up_weight, down_weight)
    rows, scaled, mine, pre_sent, pre_kept = first(pieces, up_sent, up_weight)
    grad_got = swap(act_grad_half(scaled, down_sent, BF16)[0], "tensor", 1)
    pre_sum = pre_kept + swap(pre_sent, "tensor", 1).astype(F32)
    rounded, scaled = lax.optimization_barrier((pre_sum.astype(BF16), scaled))
    grad_kept, down_kept = act_grad_half(scaled, down_kept, F32, True)
    pre = over_chips(pre_sum + swap(rounded, "tensor", 2).astype(F32), 4)
    act = jax.nn.silu(pre).astype(BF16)
    act, pre = lax.optimization_barrier((act, pre))
    act_other = swap(act, "tensor", 1)
    (down_other,) = load(down_weight, ("other",), hidden // 2, width)
    y = y_terms(act, act_other, down_kept, down_other)
    act_grad = over_chips(grad_kept + grad_got.astype(F32))
    act_grad, y = lax.optimization_barrier((act_grad, y))
    sig = jax.nn.sigmoid(pre)
    pre_grad = (act_grad * sig * (1.0 + pre * (1.0 - sig))).astype(BF16)
    pre_grad_other = swap(pre_grad, "tensor", 1)
    row_own = row_part(pre_grad, up_weight)
    terms = all_terms(pre_grad_other, row_own, y, up_weight, local)

    tile = min(256, hidden // 2, width)
    blocks = width // tile
    early = blocks // 4
    grads = (rows, pre_grad, pre_grad_other)
    down_grad, up_grad = weight_grads(
        tile, (0, early), (act, act_other, scaled, *grads), ((hidden, width), (width, hidden)), True
    )
    terms = sum_over_vit(terms.reshape(vits, seqs, 2 * local, width))
    terms, up_grad = lax.optimization_barrier((terms, up_grad))
    arrived = pieces_over_seq(terms)
    (up_grad,) = weight_grads(tile, (early, blocks), grads, ((width, hidden),), False, (up_grad,))
    mixed, token_grad = final(arrived, mine, place)
    return (mixed, token_grad, up_grad, down_grad)


def solution(mesh):
    return jax.shard_map(
        per_device,
        mesh=mesh,
        in_specs=(
            P(("vit", "seq"), "tensor"),
            P(("vit", "seq")),
            P(("vit", "seq")),
            P(("vit", "seq")),
            P("tensor", ("vit", "seq")),
            P(("vit", "seq"), "tensor"),
            P(("vit", "seq"), "tensor"),
        ),
        out_specs=(
            P(("vit", "seq"), "tensor"),
            P(("vit", "seq"), "tensor"),
            P("tensor", ("vit", "seq")),
            P(("vit", "seq"), "tensor"),
        ),
        check_vma=False,
    )
```

profile of v0, /device:TPU:0, one launch (start us, length us, event | category | flops | bytes accessed | tf_op | source)
XLA Modules:
  0.0 64.2 jit_solution(3713766301316765491)
XLA Ops:
  0.6 1.1 %route.1 = (bf16[16,2176]{1,0:T(8,128)(2,1)S(1)}, bf16[8,32]{1,0:T(8,128)(2,1)S(1)}) custom-call(s32[1,32]{1,0:T(1,128)} %bitcast.19, s32[1,32]{1,0:T(1,128)} %bitcast.20, f32[1,32]{1,0:T(1,128)} %bitcast.21, bf16[32,2048]{1,0:T(8,128)(2,1)} %refs_3_.1, bf16[8,2048]{1,0:T(8,128)(2,1)} %refs_4_.1), custom_call_target="tpu_custom_call" | custom-call | tf_op jit(solution)/shard_map/route/pallas_call | solution.py:162
  1.8 3.1 %collective-permute-start = (bf16[16,2176]{1,0:T(8,128)(2,1)S(1)}, bf16[16,2176]{1,0:T(8,128)(2,1)S(1)}, u32[]{:S(2)}, u32[]{:S(2)}) collective-permute-start(bf16[16,2176]{1,0:T(8,128)(2,1)S(1)} %get-tuple-element.42.refs_0_), channel_id=1, source_target_pairs={{0,4},{4,0},{8,12},{12,8},{1,5},{5,1},{9,13},{13,9},{2,6},{6,2},{1... | collective-permute-start | bytes 208904 | tf_op jit(solution)/shard_map/ppermute | solution.py:45
  4.9 2.5 %collective-permute-start.2 = (bf16[16,2176]{1,0:T(8,128)(2,1)S(1)}, bf16[16,2176]{1,0:T(8,128)(2,1)S(1)}, u32[]{:S(2)}, u32[]{:S(2)}) collective-permute-start(bf16[16,2176]{1,0:T(8,128)(2,1)S(1)} %get-tuple-element.42.refs_0_), channel_id=1, source_target_pairs={{0,12},{4,8},{8,4},{12,0},{1,13},{5,9},{9,5},{13,1},{2,14},{6,10},... | collective-permute-start | bytes 208904 | tf_op jit(solution)/shard_map/ppermute | solution.py:45
  7.4 0.1 collective-permute-start.1
  7.5 0.0 collective-permute-done.refs_1_
  7.5 1.7 %collective-permute-start.3 = (bf16[16,2176]{1,0:T(8,128)(2,1)S(1)}, bf16[16,2176]{1,0:T(8,128)(2,1)S(1)}, u32[]{:S(2)}, u32[]{:S(2)}) collective-permute-start(bf16[16,2176]{1,0:T(8,128)(2,1)S(1)} %get-tuple-element.42.refs_0_), channel_id=1, source_target_pairs={{0,16},{16,0},{1,17},{17,1},{2,18},{18,2},{3,19},{19,3},{4,20},{20... | collective-permute-start | bytes 208904 | tf_op jit(solution)/shard_map/ppermute | solution.py:45
  9.2 0.4 collective-permute-start.4
  9.5 2.2 %load.4.refs_8_ = bf16[2048,1024]{1,0:T(8,128)(2,1)S(1)} custom-call(bf16[2048,2048]{1,0:T(8,128)(2,1)} %up.3), custom_call_target="tpu_custom_call" | custom-call | bytes 4194304 | tf_op jit(solution)/shard_map/load/pallas_call | solution.py:77
  11.7 2.2 %load.5.down = bf16[1024,2048]{1,0:T(8,128)(2,1)S(1)} custom-call(bf16[2048,2048]{1,0:T(8,128)(2,1)} %refs_0_.4), custom_call_target="tpu_custom_call" | custom-call | bytes 4194304 | tf_op jit(solution)/shard_map/load/pallas_call | solution.py:77
  14.0 0.2 collective-permute-done.1.refs_2_
  14.1 1.6 %collective-permute-start.5 = (bf16[16,2176]{1,0:T(8,128)(2,1)S(1)}, bf16[16,2176]{1,0:T(8,128)(2,1)S(1)}, u32[]{:S(2)}, u32[]{:S(2)}) collective-permute-start(bf16[16,2176]{1,0:T(8,128)(2,1)S(1)} %collective-permute-done.1.refs_2_), channel_id=1, source_target_pairs={{0,16},{16,0},{1,17},{17,1},{2,18},{18,2},{3,19},{19,3},{4,20},{20... | collective-permute-start | bytes 208904 | tf_op jit(solution)/shard_map/ppermute | solution.py:45
  15.7 0.5 collective-permute-start.6
  16.2 2.2 %load.6.down = bf16[1024,2048]{1,0:T(8,128)(2,1)S(1)} custom-call(bf16[2048,2048]{1,0:T(8,128)(2,1)} %refs_0_.4), custom_call_target="tpu_custom_call" | custom-call | bytes 4194304 | tf_op jit(solution)/shard_map/load/pallas_call | solution.py:77
  18.4 0.0 collective-permute-done.3.refs_4_
  18.4 0.0 collective-permute-done.4.refs_5_
  18.4 0.6 collective-permute-done.5.refs_6_
  19.0 1.0 %collective-permute-done.6.refs_7_ = bf16[16,2176]{1,0:T(8,128)(2,1)S(1)} collective-permute-done((bf16[16,2176]{1,0:T(8,128)(2,1)S(1)}, bf16[16,2176]{1,0:T(8,128)(2,1)S(1)}, u32[]{:S(2)}, u32[]{:S(2)}) %collective-permute-start.6) | collective-permute-done | bytes 69664 | tf_op jit(solution)/shard_map/ppermute | solution.py:45
  20.0 2.9 %first.1 = (bf16[64,2048]{1,0:T(8,128)(2,1)S(1)}, bf16[64,2048]{1,0:T(8,128)(2,1)S(1)}, bf16[16,2176]{1,0:T(8,128)(2,1)S(1)}, bf16[64,1024]{1,0:T(8,128)(2,1)S(1)}, f32[64,1024]{1,0:T(8,128)S(1)}) custom-call(bf16[16,2176]{1,0:T(8,128)(2,1)S(1)} %get-tuple-element.42.refs_0_, bf16[16,2176]{1,0:T(8,128)(2,1)S(1)} %collective-permute-done.refs_1_, ...), custom_call_target="tpu_custom_call" | custom-call | flops 536870912 | bytes 8388608 | tf_op jit(solution)/shard_map/first/pallas_call | solution.py:227
  23.0 0.1 collective-permute-start.7
  23.0 2.2 %load.7.down_other = bf16[1024,2048]{1,0:T(8,128)(2,1)S(1)} custom-call(bf16[2048,2048]{1,0:T(8,128)(2,1)} %refs_0_.4), custom_call_target="tpu_custom_call" | custom-call | bytes 4194304 | tf_op jit(solution)/shard_map/load/pallas_call | solution.py:77
  25.3 1.5 %act_grad.3 = bf16[64,1024]{1,0:T(8,128)(2,1)S(1)} custom-call(bf16[64,2048]{1,0:T(8,128)(2,1)S(1)} %get-tuple-element.55.scaled.refs_2_, bf16[1024,2048]{1,0:T(8,128)(2,1)S(1)} %load.5.down), custom_call_target="tpu_custom_call" | custom-call | flops 268435456 | bytes 4194304 | tf_op jit(solution)/shard_map/act_grad/pallas_call | solution.py:256
  26.8 0.6 collective-permute-start.8
  27.4 1.6 %collective-permute-start.10 = (bf16[64,1024]{1,0:T(8,128)(2,1)S(1)}, bf16[64,1024]{1,0:T(8,128)(2,1)S(1)}, u32[]{:S(2)}, u32[]{:S(2)}) collective-permute-start(bf16[64,1024]{1,0:T(8,128)(2,1)S(1)} %fusion.1), channel_id=1, source_target_pairs={{0,2},{1,3},{2,0},{3,1},{4,6},{5,7},{6,4},{7,5},{8,10},{9,11},{10,... | collective-permute-start | bytes 393224 | tf_op jit(solution)/shard_map/ppermute | solution.py:45
  28.9 1.8 %act_grad.2 = (f32[64,1024]{1,0:T(8,128)S(1)}, bf16[1024,2048]{1,0:T(8,128)(2,1)S(1)}) custom-call(bf16[64,2048]{1,0:T(8,128)(2,1)S(1)} %get-tuple-element.55.scaled.refs_2_, bf16[1024,2048]{1,0:T(8,128)(2,1)S(1)} %load.6.down), custom_call_target="tpu_custom_call" | custom-call | flops 268435456 | bytes 4194304 | tf_op jit(solution)/shard_map/act_grad/pallas_call | solution.py:256
  30.8 0.0 collective-permute-done.8
  30.8 0.6 collective-permute-start.9
  31.4 1.5 %collective-permute-done.10 = bf16[64,1024]{1,0:T(8,128)(2,1)S(1)} collective-permute-done((bf16[64,1024]{1,0:T(8,128)(2,1)S(1)}, bf16[64,1024]{1,0:T(8,128)(2,1)S(1)}, u32[]{:S(2)}, u32[]{:S(2)}) %collective-permute-start.10) | collective-permute-done | bytes 131104 | tf_op jit(solution)/shard_map/ppermute | solution.py:45
  32.9 0.1 multiply_convert_fusion.1
  33.0 0.1 collective-permute-start.11
  33.1 3.0 %collective-permute-done.9 = bf16[64,1024]{1,0:T(8,128)(2,1)S(1)} collective-permute-done((bf16[64,1024]{1,0:T(8,128)(2,1)S(1)}, bf16[64,1024]{1,0:T(8,128)(2,1)S(1)}, u32[]{:S(2)}, u32[]{:S(2)}) %collective-permute-start.9) | collective-permute-done | bytes 131104 | tf_op jit(solution)/shard_map/ppermute | solution.py:45
  36.0 0.1 convert_add_fusion.2
  36.1 0.0 collective-permute-done.11.other.refs_1_
  36.1 1.6 %y.1 = bf16[64,2048]{1,0:T(8,128)(2,1)S(1)} custom-call(bf16[64,1024]{1,0:T(8,128)(2,1)S(1)} %get-tuple-element.60.own.refs_0_, bf16[64,1024]{1,0:T(8,128)(2,1)S(1)} %collective-permute-done.11.other.refs_1_, bf16[1024,2048]{1,0:T(8,128)(2,1)S(1)} %get-tuple-element.61.down_own, bf16[1024,2048]{1,0:T(8,128)(2,1)S(1)} %load.7.down_other), custom_call_target="tpu_custom_call" | custom-call | flops 536870912 | bytes 8388608 | tf_op jit(solution)/shard_map/y/pallas_call | solution.py:313
  37.7 0.1 multiply_convert_fusion.own.refs_4_.refs_1_
  37.8 0.1 collective-permute-start.12
  37.9 3.0 %row_part.1.before = f32[64,2048]{1,0:T(8,128)S(1)} custom-call(bf16[64,1024]{1,0:T(8,128)(2,1)S(1)} %multiply_convert_fusion.own.refs_4_.refs_1_, bf16[2048,2048]{1,0:T(8,128)(2,1)} %up.3), custom_call_target="tpu_custom_call" | custom-call | flops 268435456 | bytes 4194304 | tf_op jit(solution)/shard_map/row_part/pallas_call | solution.py:336
  40.9 3.7 %all_terms.1 = bf16[128,2048]{1,0:T(8,128)(2,1)S(1)} custom-call(bf16[64,1024]{1,0:T(8,128)(2,1)S(1)} %collective-permute-done.12.other.refs_5_.refs_2_, f32[64,2048]{1,0:T(8,128)S(1)} %row_part.1.before, bf16[64,2048]{1,0:T(8,128)(2,1)S(1)} %y.1, bf16[2048,2048]{1,0:T(8,128)(2,1)} %up.3), custom_call_target="tpu_custom_call" | custom-call | flops 268435456 | bytes 4194304 | tf_op jit(solution)/shard_map/all_terms/pallas_call | solution.py:370
  44.7 1.2 %collective-permute-start.13 = (bf16[4,16,2048]{2,1,0:T(8,128)(2,1)S(1)}, bf16[4,16,2048]{2,1,0:T(8,128)(2,1)S(1)}, u32[]{:S(2)}, u32[]{:S(2)}) collective-permute-start(bf16[4,16,2048]{2,1,0:T(8,128)(2,1)S(1)} %dynamic-slice_bitcast_fusion), channel_id=1, source_target_pairs={{0,16},{16,0},{1,17},{17,1},{2,18},{18,2},{3,19},{19,3},{4,20},{20... | collective-permute-start | bytes 786440 | tf_op jit(solution)/shard_map/ppermute | solution.py:45
  45.9 7.6 %weight_grads.2 = (f32[2048,2048]{1,0:T(8,128)}, f32[2048,2048]{1,0:T(8,128)}) custom-call(bf16[64,1024]{1,0:T(8,128)(2,1)S(1)} %get-tuple-element.60.own.refs_0_, bf16[64,1024]{1,0:T(8,128)(2,1)S(1)} %collective-permute-done.11.other.refs_1_, bf16[64,2048]{1,0:T(8,128)(2,1)S(1)} %get-tuple-element.55.scaled.refs_2_, ...), custom_call_target="tpu_custom_call" | custom-call | flops 1073741824 | bytes 25165824 | tf_op jit(solution)/shard_map/weight_grads/pallas_call | solution.py:424
  53.5 0.1 fusion
  53.6 3.6 %collective-permute-start.16 = (bf16[16,2048]{1,0:T(8,128)(2,1)S(1)}, bf16[16,2048]{1,0:T(8,128)(2,1)S(1)}, u32[]{:S(2)}, u32[]{:S(2)}) collective-permute-start(bf16[16,2048]{1,0:T(8,128)(2,1)S(1)} %get-tuple-element.76), channel_id=1, source_target_pairs={{0,12},{4,8},{8,4},{12,0},{1,13},{5,9},{9,5},{13,1},{2,14},{6,10},... | collective-permute-start | bytes 196616 | tf_op jit(solution)/shard_map/ppermute | solution.py:45
  57.2 0.0 collective-permute-start.15
  57.2 0.9 %collective-permute-start.14 = (bf16[16,2048]{1,0:T(8,128)(2,1)S(1)}, bf16[16,2048]{1,0:T(8,128)(2,1)S(1)}, u32[]{:S(2)}, u32[]{:S(2)}) collective-permute-start(bf16[16,2048]{1,0:T(8,128)(2,1)S(1)} %get-tuple-element.78), channel_id=1, source_target_pairs={{0,4},{4,0},{8,12},{12,8},{1,5},{5,1},{9,13},{13,9},{2,6},{6,2},{1... | collective-permute-start | bytes 196616 | tf_op jit(solution)/shard_map/ppermute | solution.py:45
  58.1 5.1 %weight_grads.3 = f32[2048,2048]{1,0:T(8,128)} custom-call(bf16[64,2048]{1,0:T(8,128)(2,1)S(1)} %get-tuple-element.65.refs_3_.refs_0_, bf16[64,1024]{1,0:T(8,128)(2,1)S(1)} %multiply_convert_fusion.own.refs_4_.refs_1_, bf16[64,1024]{1,0:T(8,128)(2,1)S(1)} %collective-permute-done.12.other.refs_5_.refs_2_, ...), custom_call_target="tpu_custom_call", output_to_operand_aliasing={{}: (3, {})} | custom-call | flops 536870912 | bytes 12582912 | tf_op jit(solution)/shard_map/weight_grads/pallas_call | solution.py:424
  63.1 0.0 collective-permute-done.16.refs_3_
  63.2 0.1 collective-permute-done.15.refs_2_
  63.3 0.0 collective-permute-done.14.refs_1_
  63.3 0.9 %final.1 = (bf16[8,2048]{1,0:T(8,128)(2,1)}, bf16[32,2048]{1,0:T(8,128)(2,1)}) custom-call(bf16[16,2048]{1,0:T(8,128)(2,1)S(1)} %get-tuple-element.79.refs_0_, bf16[16,2048]{1,0:T(8,128)(2,1)S(1)} %collective-permute-done.14.refs_1_, bf16[16,2048]{1,0:T(8,128)(2,1)S(1)} %collective-permute-done.15.refs_2_, ...), custom_call_target="tpu_custom_call" | custom-call | tf_op jit(solution)/shard_map/final/pallas_call | solution.py:458
  (8 shorter events, 0.1 us)
Async XLA Ops:
  1.8 5.7 %collective-permute-start = (bf16[16,2176]{1,0:T(8,128)(2,1)S(1)}, bf16[16,2176]{1,0:T(8,128)(2,1)S(1)}, u32[]{:S(2)}, u32[]{:S(2)}) collective-permute-start(bf16[16,2176]{1,0:T(8,128)(2,1)S(1)} %get-tuple-element.42.refs_0_), channel_id=1, source_target_pairs={{0,4},{4,0},{8,12},{12,8},{1,5},{5,1},{9,13},{13,9},{2,6},{6,2},{1... | collective-permute-start | bytes 208904 | tf_op jit(solution)/shard_map/ppermute | solution.py:45
  4.9 9.1 %collective-permute-start.2 = (bf16[16,2176]{1,0:T(8,128)(2,1)S(1)}, bf16[16,2176]{1,0:T(8,128)(2,1)S(1)}, u32[]{:S(2)}, u32[]{:S(2)}) collective-permute-start(bf16[16,2176]{1,0:T(8,128)(2,1)S(1)} %get-tuple-element.42.refs_0_), channel_id=1, source_target_pairs={{0,12},{4,8},{8,4},{12,0},{1,13},{5,9},{9,5},{13,1},{2,14},{6,10},... | collective-permute-start | bytes 208904 | tf_op jit(solution)/shard_map/ppermute | solution.py:45
  7.4 6.8 %collective-permute-start.1 = (bf16[16,2176]{1,0:T(8,128)(2,1)S(1)}, bf16[16,2176]{1,0:T(8,128)(2,1)S(1)}, u32[]{:S(2)}, u32[]{:S(2)}) collective-permute-start(bf16[16,2176]{1,0:T(8,128)(2,1)S(1)} %get-tuple-element.42.refs_0_), channel_id=1, source_target_pairs={{0,8},{4,12},{8,0},{12,4},{1,9},{5,13},{9,1},{13,5},{2,10},{6,14},... | collective-permute-start | bytes 208904 | tf_op jit(solution)/shard_map/ppermute | solution.py:45
  7.5 10.9 %collective-permute-start.3 = (bf16[16,2176]{1,0:T(8,128)(2,1)S(1)}, bf16[16,2176]{1,0:T(8,128)(2,1)S(1)}, u32[]{:S(2)}, u32[]{:S(2)}) collective-permute-start(bf16[16,2176]{1,0:T(8,128)(2,1)S(1)} %get-tuple-element.42.refs_0_), channel_id=1, source_target_pairs={{0,16},{16,0},{1,17},{17,1},{2,18},{18,2},{3,19},{19,3},{4,20},{20... | collective-permute-start | bytes 208904 | tf_op jit(solution)/shard_map/ppermute | solution.py:45
  9.2 9.2 %collective-permute-start.4 = (bf16[16,2176]{1,0:T(8,128)(2,1)S(1)}, bf16[16,2176]{1,0:T(8,128)(2,1)S(1)}, u32[]{:S(2)}, u32[]{:S(2)}) collective-permute-start(bf16[16,2176]{1,0:T(8,128)(2,1)S(1)} %collective-permute-done.refs_1_), channel_id=1, source_target_pairs={{0,16},{16,0},{1,17},{17,1},{2,18},{18,2},{3,19},{19,3},{4,20},{20... | collective-permute-start | bytes 208904 | tf_op jit(solution)/shard_map/ppermute | solution.py:45
  14.1 4.9 %collective-permute-start.5 = (bf16[16,2176]{1,0:T(8,128)(2,1)S(1)}, bf16[16,2176]{1,0:T(8,128)(2,1)S(1)}, u32[]{:S(2)}, u32[]{:S(2)}) collective-permute-start(bf16[16,2176]{1,0:T(8,128)(2,1)S(1)} %collective-permute-done.1.refs_2_), channel_id=1, source_target_pairs={{0,16},{16,0},{1,17},{17,1},{2,18},{18,2},{3,19},{19,3},{4,20},{20... | collective-permute-start | bytes 208904 | tf_op jit(solution)/shard_map/ppermute | solution.py:45
  15.7 4.3 %collective-permute-start.6 = (bf16[16,2176]{1,0:T(8,128)(2,1)S(1)}, bf16[16,2176]{1,0:T(8,128)(2,1)S(1)}, u32[]{:S(2)}, u32[]{:S(2)}) collective-permute-start(bf16[16,2176]{1,0:T(8,128)(2,1)S(1)} %collective-permute-done.2.refs_3_), channel_id=1, source_target_pairs={{0,16},{16,0},{1,17},{17,1},{2,18},{18,2},{3,19},{19,3},{4,20},{20... | collective-permute-start | bytes 208904 | tf_op jit(solution)/shard_map/ppermute | solution.py:45
  23.0 4.4 %collective-permute-start.7 = (bf16[64,1024]{1,0:T(8,128)(2,1)S(1)}, bf16[64,1024]{1,0:T(8,128)(2,1)S(1)}, u32[]{:S(2)}, u32[]{:S(2)}) collective-permute-start(bf16[64,1024]{1,0:T(8,128)(2,1)S(1)} %get-tuple-element.53), channel_id=1, source_target_pairs={{0,1},{1,0},{2,3},{3,2},{4,5},{5,4},{6,7},{7,6},{8,9},{9,8},{10,11... | collective-permute-start | bytes 393224 | tf_op jit(solution)/shard_map/ppermute | solution.py:45
  26.8 4.0 %collective-permute-start.8 = (bf16[64,1024]{1,0:T(8,128)(2,1)S(1)}, bf16[64,1024]{1,0:T(8,128)(2,1)S(1)}, u32[]{:S(2)}, u32[]{:S(2)}) collective-permute-start(bf16[64,1024]{1,0:T(8,128)(2,1)S(1)} %act_grad.3), channel_id=1, source_target_pairs={{0,1},{1,0},{2,3},{3,2},{4,5},{5,4},{6,7},{7,6},{8,9},{9,8},{10,11... | collective-permute-start | bytes 393224 | tf_op jit(solution)/shard_map/ppermute | solution.py:45
  27.4 5.5 %collective-permute-start.10 = (bf16[64,1024]{1,0:T(8,128)(2,1)S(1)}, bf16[64,1024]{1,0:T(8,128)(2,1)S(1)}, u32[]{:S(2)}, u32[]{:S(2)}) collective-permute-start(bf16[64,1024]{1,0:T(8,128)(2,1)S(1)} %fusion.1), channel_id=1, source_target_pairs={{0,2},{1,3},{2,0},{3,1},{4,6},{5,7},{6,4},{7,5},{8,10},{9,11},{10,... | collective-permute-start | bytes 393224 | tf_op jit(solution)/shard_map/ppermute | solution.py:45
  30.8 5.2 %collective-permute-start.9 = (bf16[64,1024]{1,0:T(8,128)(2,1)S(1)}, bf16[64,1024]{1,0:T(8,128)(2,1)S(1)}, u32[]{:S(2)}, u32[]{:S(2)}) collective-permute-start(bf16[64,1024]{1,0:T(8,128)(2,1)S(1)} %fusion.2), channel_id=1, source_target_pairs={{0,2},{1,3},{2,0},{3,1},{4,6},{5,7},{6,4},{7,5},{8,10},{9,11},{10,... | collective-permute-start | bytes 393224 | tf_op jit(solution)/shard_map/ppermute | solution.py:45
  33.0 3.1 %collective-permute-start.11 = (bf16[64,1024]{1,0:T(8,128)(2,1)S(1)}, bf16[64,1024]{1,0:T(8,128)(2,1)S(1)}, u32[]{:S(2)}, u32[]{:S(2)}) collective-permute-start(bf16[64,1024]{1,0:T(8,128)(2,1)S(1)} %get-tuple-element.60.own.refs_0_), channel_id=1, source_target_pairs={{0,1},{1,0},{2,3},{3,2},{4,5},{5,4},{6,7},{7,6},{8,9},{9,8},{10,11... | collective-permute-start | bytes 393224 | tf_op jit(solution)/shard_map/ppermute | solution.py:45
  37.8 3.1 %collective-permute-start.12 = (bf16[64,1024]{1,0:T(8,128)(2,1)S(1)}, bf16[64,1024]{1,0:T(8,128)(2,1)S(1)}, u32[]{:S(2)}, u32[]{:S(2)}) collective-permute-start(bf16[64,1024]{1,0:T(8,128)(2,1)S(1)} %multiply_convert_fusion.own.refs_4_.refs_1_), channel_id=1, source_target_pairs={{0,1},{1,0},{2,3},{3,2},{4,5},{5,4},{6,7},{7,6},{8,9},{9,8},{10,11... | collective-permute-start | bytes 393224 | tf_op jit(solution)/shard_map/ppermute | solution.py:45
  44.7 8.8 %collective-permute-start.13 = (bf16[4,16,2048]{2,1,0:T(8,128)(2,1)S(1)}, bf16[4,16,2048]{2,1,0:T(8,128)(2,1)S(1)}, u32[]{:S(2)}, u32[]{:S(2)}) collective-permute-start(bf16[4,16,2048]{2,1,0:T(8,128)(2,1)S(1)} %dynamic-slice_bitcast_fusion), channel_id=1, source_target_pairs={{0,16},{16,0},{1,17},{17,1},{2,18},{18,2},{3,19},{19,3},{4,20},{20... | collective-permute-start | bytes 786440 | tf_op jit(solution)/shard_map/ppermute | solution.py:45
  53.6 9.5 %collective-permute-start.16 = (bf16[16,2048]{1,0:T(8,128)(2,1)S(1)}, bf16[16,2048]{1,0:T(8,128)(2,1)S(1)}, u32[]{:S(2)}, u32[]{:S(2)}) collective-permute-start(bf16[16,2048]{1,0:T(8,128)(2,1)S(1)} %get-tuple-element.76), channel_id=1, source_target_pairs={{0,12},{4,8},{8,4},{12,0},{1,13},{5,9},{9,5},{13,1},{2,14},{6,10},... | collective-permute-start | bytes 196616 | tf_op jit(solution)/shard_map/ppermute | solution.py:45
  57.2 6.1 %collective-permute-start.15 = (bf16[16,2048]{1,0:T(8,128)(2,1)S(1)}, bf16[16,2048]{1,0:T(8,128)(2,1)S(1)}, u32[]{:S(2)}, u32[]{:S(2)}) collective-permute-start(bf16[16,2048]{1,0:T(8,128)(2,1)S(1)} %get-tuple-element.77), channel_id=1, source_target_pairs={{0,8},{4,12},{8,0},{12,4},{1,9},{5,13},{9,1},{13,5},{2,10},{6,14},... | collective-permute-start | bytes 196616 | tf_op jit(solution)/shard_map/ppermute | solution.py:45
  57.2 6.1 %collective-permute-start.14 = (bf16[16,2048]{1,0:T(8,128)(2,1)S(1)}, bf16[16,2048]{1,0:T(8,128)(2,1)S(1)}, u32[]{:S(2)}, u32[]{:S(2)}) collective-permute-start(bf16[16,2048]{1,0:T(8,128)(2,1)S(1)} %get-tuple-element.78), channel_id=1, source_target_pairs={{0,4},{4,0},{8,12},{12,8},{1,5},{5,1},{9,13},{13,9},{2,6},{6,2},{1... | collective-permute-start | bytes 196616 | tf_op jit(solution)/shard_map/ppermute | solution.py:45
where the time goes:
time: 64.3 us; the launch traced here: 64.2 us
  Pallas kernels  38.1 us (59%)
  starting transfers between devices  18.3 us (28%)
  waiting for transfers between devices  6.37 us (10%)
  between operations  0.88 us (1%)
    ppermute x17, starting transfers between devices, swap(): return lax.ppermute(value, axis, [(i, i ^ bit) for i in range(size)])  18.3 us
    pallas_call x2, Pallas kernels, weight_grads(): pl.pallas_call(functools.partial(weight_grads_kernel, ahead, begin), out_...  12.7 us
    pallas_call x4, Pallas kernels, load(): pl.pallas_call(functools.partial(load_kernel, wheres), out_shape=[pltpu.V...  8.85 us
    ppermute x17, waiting for transfers between devices, swap(): return lax.ppermute(value, axis, [(i, i ^ bit) for i in range(size)])  6.37 us
    pallas_call x1, Pallas kernels, all_terms(): pl.pallas_call(functools.partial(terms_kernel, lax.axis_size('seq'), loca...  3.71 us
    pallas_call x2, Pallas kernels, act_grad_half(): pl.pallas_call(act_grad_kernel, out_shape=[held((slots, half), dtype)] +...  3.36 us
    pallas_call x1, Pallas kernels, row_part(): pl.pallas_call(row_kernel, out_shape=held((slots, width), F32), in_specs=...  3.03 us
    pallas_call x1, Pallas kernels, first(): pl.pallas_call(functools.partial(first_kernel, lax.axis_size('seq'), coun...  2.92 us
  transfers between devices with their start and end apart: 17, of which 6 were waited for; matrix products, arithmetic and copies ran while one was open for 0% of the time, Pallas kernels for 43%

commit v1 on v0

--- a/solution.py
+++ b/solution.py
@@ -86,22 +86,36 @@
     )(in_hbm(weights))
 
 
-def gather_pieces(piece, up, down):
+def tick_kernel(value, same):
+    same[...] = value[...]
+
+
+def tick(value):
+    return pl.pallas_call(
+        tick_kernel,
+        out_shape=held(value.shape, value.dtype),
+        in_specs=[IN_VMEM],
+        out_specs=IN_VMEM,
+        compiler_params=params(1),
+        name="tick",
+    )(value)
+
+
+def gather_pieces(piece, up, down, place):
     seqs, vits = lax.axis_size("seq"), lax.axis_size("vit")
     deep, hidden = up.shape
     piece, up = lax.optimization_barrier((piece, up))
     along = [piece] + [swap(piece, "seq", k) for k in range(1, seqs)]
-    near = along[: seqs // 2]
-    near, up, down = lax.optimization_barrier((near, up, down))
     (up,) = load(up, ("other",), deep, hidden // 2)
-    (sent,) = load(down, ("other",), hidden // 2, deep)
-    far, up, sent, down = lax.optimization_barrier((along[seqs // 2 :], up, sent, down))
-    along = near + far
+    near, up, place = lax.optimization_barrier((along[1 : seqs // 2], up, place))
+    place = tick(place)
+    far, up, down, place = lax.optimization_barrier((along[seqs // 2 :], up, down, place))
+    along = [piece] + near + far
     out = list(along)
     for v in range(1, vits):
         out += [swap(p, "vit", v) for p in along]
-    (kept,) = load(down, ("own",), hidden // 2, deep)
-    return (out, *lax.optimization_barrier((up, sent, kept)))
+    sent, kept = load(down, ("other", "own"), hidden // 2, deep)
+    return (out, place, *lax.optimization_barrier((up, sent, kept)))
 
 
 def sum_over_vit(blocks):
@@ -477,7 +491,7 @@
     seqs, vits = lax.axis_size("seq"), lax.axis_size("vit")
     hidden = up_weight.shape[1]
     piece, place = route(positions, picked, router_score, merged, mixed_grad)
-    pieces, up_sent, down_sent, down_kept = gather_pieces(piece, up_weight, down_weight)
+    pieces, place, up_sent, down_sent, down_kept = gather_pieces(piece, up_weight, down_weight, place)
     rows, scaled, mine, pre_sent, pre_kept = first(pieces, up_sent, up_weight)
     grad_got = swap(act_grad_half(scaled, down_sent, BF16)[0], "tensor", 1)
     pre_sum = pre_kept + swap(pre_sent, "tensor", 1).astype(F32)

time: 64.3 us -> 65.7 us (1.022)
  waiting for transfers between devices: 6.37 us -> 7.58 us
  starting transfers between devices: 18.3 us -> 19.4 us
  Pallas kernels: 38.1 us -> 37.2 us
    ppermute x17, waiting for transfers between devices: 6.37 us -> 7.58 us  [swap(): return lax.ppermute(value, axis, [(i, i ^ bit) for i in range(size)])]
    ppermute x17, starting transfers between devices: 18.3 us -> 19.4 us  [swap(): return lax.ppermute(value, axis, [(i, i ^ bit) for i in range(size)])]
    pallas_call x4 -> x3, Pallas kernels: 8.85 us -> 7.9 us  [load(): pl.pallas_call(functools.partial(load_kernel, wheres), out_shape=[pltpu.V...]
  transfers between devices with their start and end apart: 17 -> 17, of which waited for: 6 -> 5; matrix products, arithmetic and copies ran while one was open for 0% -> 0% of each run, Pallas kernels for 43% -> 41%
where the time goes in v1:
time: 65.7 us; the launch traced here: 65.5 us
  Pallas kernels  37.2 us (57%)
  starting transfers between devices  19.4 us (30%)
  waiting for transfers between devices  7.58 us (12%)
  between operations  0.9 us (1%)
    ppermute x17, starting transfers between devices, swap(): return lax.ppermute(value, axis, [(i, i ^ bit) for i in range(size)])  19.4 us
    pallas_call x2, Pallas kernels, weight_grads(): pl.pallas_call(functools.partial(weight_grads_kernel, ahead, begin), out_...  12.7 us
    pallas_call x3, Pallas kernels, load(): pl.pallas_call(functools.partial(load_kernel, wheres), out_shape=[pltpu.V...  7.9 us
    ppermute x17, waiting for transfers between devices, swap(): return lax.ppermute(value, axis, [(i, i ^ bit) for i in range(size)])  7.58 us
    pallas_call x1, Pallas kernels, all_terms(): pl.pallas_call(functools.partial(terms_kernel, lax.axis_size('seq'), loca...  3.71 us
    pallas_call x2, Pallas kernels, act_grad_half(): pl.pallas_call(act_grad_kernel, out_shape=[held((slots, half), dtype)] +...  3.36 us
    pallas_call x1, Pallas kernels, row_part(): pl.pallas_call(row_kernel, out_shape=held((slots, width), F32), in_specs=...  3.03 us
    pallas_call x1, Pallas kernels, first(): pl.pallas_call(functools.partial(first_kernel, lax.axis_size('seq'), coun...  2.92 us
  transfers between devices with their start and end apart: 17, of which 5 were waited for; matrix products, arithmetic and copies ran while one was open for 0% of the time, Pallas kernels for 41%

profile of v1, /device:TPU:0, one launch (start us, length us, event | category | flops | bytes accessed | tf_op | source)
XLA Modules:
  0.0 65.5 jit_solution(7179540182421681439)
XLA Ops:
  0.6 1.1 %route.1 = (bf16[16,2176]{1,0:T(8,128)(2,1)S(1)}, bf16[8,32]{1,0:T(8,128)(2,1)S(1)}) custom-call(s32[1,32]{1,0:T(1,128)} %bitcast.19, s32[1,32]{1,0:T(1,128)} %bitcast.20, f32[1,32]{1,0:T(1,128)} %bitcast.21, bf16[32,2048]{1,0:T(8,128)(2,1)} %refs_3_.1, bf16[8,2048]{1,0:T(8,128)(2,1)} %refs_4_.1), custom_call_target="tpu_custom_call" | custom-call | tf_op jit(solution)/shard_map/route/pallas_call | solution.py:176
  1.8 3.1 %collective-permute-start = (bf16[16,2176]{1,0:T(8,128)(2,1)S(1)}, bf16[16,2176]{1,0:T(8,128)(2,1)S(1)}, u32[]{:S(2)}, u32[]{:S(2)}) collective-permute-start(bf16[16,2176]{1,0:T(8,128)(2,1)S(1)} %get-tuple-element.41.refs_0_), channel_id=1, source_target_pairs={{0,4},{4,0},{8,12},{12,8},{1,5},{5,1},{9,13},{13,9},{2,6},{6,2},{1... | collective-permute-start | bytes 208904 | tf_op jit(solution)/shard_map/ppermute | solution.py:45
  4.9 2.5 %collective-permute-start.2 = (bf16[16,2176]{1,0:T(8,128)(2,1)S(1)}, bf16[16,2176]{1,0:T(8,128)(2,1)S(1)}, u32[]{:S(2)}, u32[]{:S(2)}) collective-permute-start(bf16[16,2176]{1,0:T(8,128)(2,1)S(1)} %get-tuple-element.41.refs_0_), channel_id=1, source_target_pairs={{0,12},{4,8},{8,4},{12,0},{1,13},{5,9},{9,5},{13,1},{2,14},{6,10},... | collective-permute-start | bytes 208904 | tf_op jit(solution)/shard_map/ppermute | solution.py:45
  7.4 0.1 collective-permute-start.1
  7.5 1.5 %collective-permute-start.3 = (bf16[16,2176]{1,0:T(8,128)(2,1)S(1)}, bf16[16,2176]{1,0:T(8,128)(2,1)S(1)}, u32[]{:S(2)}, u32[]{:S(2)}) collective-permute-start(bf16[16,2176]{1,0:T(8,128)(2,1)S(1)} %get-tuple-element.41.refs_0_), channel_id=1, source_target_pairs={{0,16},{16,0},{1,17},{17,1},{2,18},{18,2},{3,19},{19,3},{4,20},{20... | collective-permute-start | bytes 208904 | tf_op jit(solution)/shard_map/ppermute | solution.py:45
  9.0 2.2 %load.3.refs_8_ = bf16[2048,1024]{1,0:T(8,128)(2,1)S(1)} custom-call(bf16[2048,2048]{1,0:T(8,128)(2,1)} %up.3), custom_call_target="tpu_custom_call" | custom-call | bytes 4194304 | tf_op jit(solution)/shard_map/load/pallas_call | solution.py:77
  11.2 0.0 collective-permute-done.refs_1_
  11.2 0.7 %collective-permute-done.2.refs_3_ = bf16[16,2176]{1,0:T(8,128)(2,1)S(1)} collective-permute-done((bf16[16,2176]{1,0:T(8,128)(2,1)S(1)}, bf16[16,2176]{1,0:T(8,128)(2,1)S(1)}, u32[]{:S(2)}, u32[]{:S(2)}) %collective-permute-start.2) | collective-permute-done | bytes 69664 | tf_op jit(solution)/shard_map/ppermute | solution.py:45
  11.9 2.2 %collective-permute-done.1.refs_2_ = bf16[16,2176]{1,0:T(8,128)(2,1)S(1)} collective-permute-done((bf16[16,2176]{1,0:T(8,128)(2,1)S(1)}, bf16[16,2176]{1,0:T(8,128)(2,1)S(1)}, u32[]{:S(2)}, u32[]{:S(2)}) %collective-permute-start.1) | collective-permute-done | bytes 69664 | tf_op jit(solution)/shard_map/ppermute | solution.py:45
  14.1 1.5 %collective-permute-start.5 = (bf16[16,2176]{1,0:T(8,128)(2,1)S(1)}, bf16[16,2176]{1,0:T(8,128)(2,1)S(1)}, u32[]{:S(2)}, u32[]{:S(2)}) collective-permute-start(bf16[16,2176]{1,0:T(8,128)(2,1)S(1)} %collective-permute-done.1.refs_2_), channel_id=1, source_target_pairs={{0,16},{16,0},{1,17},{17,1},{2,18},{18,2},{3,19},{19,3},{4,20},{20... | collective-permute-start | bytes 208904 | tf_op jit(solution)/shard_map/ppermute | solution.py:45
  15.7 0.5 collective-permute-start.6
  16.2 1.5 %collective-permute-start.4 = (bf16[16,2176]{1,0:T(8,128)(2,1)S(1)}, bf16[16,2176]{1,0:T(8,128)(2,1)S(1)}, u32[]{:S(2)}, u32[]{:S(2)}) collective-permute-start(bf16[16,2176]{1,0:T(8,128)(2,1)S(1)} %collective-permute-done.refs_1_), channel_id=1, source_target_pairs={{0,16},{16,0},{1,17},{17,1},{2,18},{18,2},{3,19},{19,3},{4,20},{20... | collective-permute-start | bytes 208904 | tf_op jit(solution)/shard_map/ppermute | solution.py:45
  17.7 3.5 %load.4 = (bf16[1024,2048]{1,0:T(8,128)(2,1)S(1)}, bf16[1024,2048]{1,0:T(8,128)(2,1)S(1)}) custom-call(bf16[2048,2048]{1,0:T(8,128)(2,1)} %refs_0_.3), custom_call_target="tpu_custom_call" | custom-call | bytes 8388608 | tf_op jit(solution)/shard_map/load/pallas_call | solution.py:77
  21.2 0.0 collective-permute-done.3.refs_4_
  21.2 0.0 collective-permute-done.5.refs_6_
  21.2 0.0 collective-permute-done.6.refs_7_
  21.2 0.2 collective-permute-done.4.refs_5_
  21.4 2.9 %first.1 = (bf16[64,2048]{1,0:T(8,128)(2,1)S(1)}, bf16[64,2048]{1,0:T(8,128)(2,1)S(1)}, bf16[16,2176]{1,0:T(8,128)(2,1)S(1)}, bf16[64,1024]{1,0:T(8,128)(2,1)S(1)}, f32[64,1024]{1,0:T(8,128)S(1)}) custom-call(bf16[16,2176]{1,0:T(8,128)(2,1)S(1)} %get-tuple-element.41.refs_0_, bf16[16,2176]{1,0:T(8,128)(2,1)S(1)} %collective-permute-done.refs_1_, ...), custom_call_target="tpu_custom_call" | custom-call | flops 536870912 | bytes 8388608 | tf_op jit(solution)/shard_map/first/pallas_call | solution.py:241
  24.4 0.1 collective-permute-start.7
  24.4 2.2 %load.5.down_other = bf16[1024,2048]{1,0:T(8,128)(2,1)S(1)} custom-call(bf16[2048,2048]{1,0:T(8,128)(2,1)} %refs_0_.3), custom_call_target="tpu_custom_call" | custom-call | bytes 4194304 | tf_op jit(solution)/shard_map/load/pallas_call | solution.py:77
  26.7 1.5 %act_grad.3 = bf16[64,1024]{1,0:T(8,128)(2,1)S(1)} custom-call(bf16[64,2048]{1,0:T(8,128)(2,1)S(1)} %get-tuple-element.57.scaled.refs_2_, bf16[1024,2048]{1,0:T(8,128)(2,1)S(1)} %get-tuple-element.60.down), custom_call_target="tpu_custom_call" | custom-call | flops 268435456 | bytes 4194304 | tf_op jit(solution)/shard_map/act_grad/pallas_call | solution.py:270
  28.2 0.5 collective-permute-start.8
  28.7 0.0 collective-permute-done.7
  28.8 1.6 %collective-permute-start.10 = (bf16[64,1024]{1,0:T(8,128)(2,1)S(1)}, bf16[64,1024]{1,0:T(8,128)(2,1)S(1)}, u32[]{:S(2)}, u32[]{:S(2)}) collective-permute-start(bf16[64,1024]{1,0:T(8,128)(2,1)S(1)} %fusion.1), channel_id=1, source_target_pairs={{0,2},{1,3},{2,0},{3,1},{4,6},{5,7},{6,4},{7,5},{8,10},{9,11},{10,... | collective-permute-start | bytes 393224 | tf_op jit(solution)/shard_map/ppermute | solution.py:45
  30.3 1.8 %act_grad.2 = (f32[64,1024]{1,0:T(8,128)S(1)}, bf16[1024,2048]{1,0:T(8,128)(2,1)S(1)}) custom-call(bf16[64,2048]{1,0:T(8,128)(2,1)S(1)} %get-tuple-element.57.scaled.refs_2_, bf16[1024,2048]{1,0:T(8,128)(2,1)S(1)} %get-tuple-element.58.down), custom_call_target="tpu_custom_call" | custom-call | flops 268435456 | bytes 4194304 | tf_op jit(solution)/shard_map/act_grad/pallas_call | solution.py:270
  32.2 0.6 collective-permute-start.9
  32.8 1.5 %collective-permute-done.10 = bf16[64,1024]{1,0:T(8,128)(2,1)S(1)} collective-permute-done((bf16[64,1024]{1,0:T(8,128)(2,1)S(1)}, bf16[64,1024]{1,0:T(8,128)(2,1)S(1)}, u32[]{:S(2)}, u32[]{:S(2)}) %collective-permute-start.10) | collective-permute-done | bytes 131104 | tf_op jit(solution)/shard_map/ppermute | solution.py:45
  34.3 0.1 multiply_convert_fusion.1
  34.4 0.1 collective-permute-start.11
  34.5 3.0 %collective-permute-done.9 = bf16[64,1024]{1,0:T(8,128)(2,1)S(1)} collective-permute-done((bf16[64,1024]{1,0:T(8,128)(2,1)S(1)}, bf16[64,1024]{1,0:T(8,128)(2,1)S(1)}, u32[]{:S(2)}, u32[]{:S(2)}) %collective-permute-start.9) | collective-permute-done | bytes 131104 | tf_op jit(solution)/shard_map/ppermute | solution.py:45
  37.4 0.1 convert_add_fusion.2
  37.5 1.6 %y.1 = bf16[64,2048]{1,0:T(8,128)(2,1)S(1)} custom-call(bf16[64,1024]{1,0:T(8,128)(2,1)S(1)} %get-tuple-element.62.own.refs_0_, bf16[64,1024]{1,0:T(8,128)(2,1)S(1)} %collective-permute-done.11.other.refs_1_, bf16[1024,2048]{1,0:T(8,128)(2,1)S(1)} %get-tuple-element.63.down_own, bf16[1024,2048]{1,0:T(8,128)(2,1)S(1)} %load.5.down_other), custom_call_target="tpu_custom_call" | custom-call | flops 536870912 | bytes 8388608 | tf_op jit(solution)/shard_map/y/pallas_call | solution.py:327
  39.1 0.1 multiply_convert_fusion.own.refs_4_.refs_1_
  39.2 0.1 collective-permute-start.12
  39.3 3.0 %row_part.1.before = f32[64,2048]{1,0:T(8,128)S(1)} custom-call(bf16[64,1024]{1,0:T(8,128)(2,1)S(1)} %multiply_convert_fusion.own.refs_4_.refs_1_, bf16[2048,2048]{1,0:T(8,128)(2,1)} %up.3), custom_call_target="tpu_custom_call" | custom-call | flops 268435456 | bytes 4194304 | tf_op jit(solution)/shard_map/row_part/pallas_call | solution.py:350
  42.3 0.0 collective-permute-done.12.other.refs_5_.refs_2_
  42.3 3.7 %all_terms.1 = bf16[128,2048]{1,0:T(8,128)(2,1)S(1)} custom-call(bf16[64,1024]{1,0:T(8,128)(2,1)S(1)} %collective-permute-done.12.other.refs_5_.refs_2_, f32[64,2048]{1,0:T(8,128)S(1)} %row_part.1.before, bf16[64,2048]{1,0:T(8,128)(2,1)S(1)} %y.1, bf16[2048,2048]{1,0:T(8,128)(2,1)} %up.3), custom_call_target="tpu_custom_call" | custom-call | flops 268435456 | bytes 4194304 | tf_op jit(solution)/shard_map/all_terms/pallas_call | solution.py:384
  46.1 1.3 %collective-permute-start.13 = (bf16[4,16,2048]{2,1,0:T(8,128)(2,1)S(1)}, bf16[4,16,2048]{2,1,0:T(8,128)(2,1)S(1)}, u32[]{:S(2)}, u32[]{:S(2)}) collective-permute-start(bf16[4,16,2048]{2,1,0:T(8,128)(2,1)S(1)} %dynamic-slice_bitcast_fusion), channel_id=1, source_target_pairs={{0,16},{16,0},{1,17},{17,1},{2,18},{18,2},{3,19},{19,3},{4,20},{20... | collective-permute-start | bytes 786440 | tf_op jit(solution)/shard_map/ppermute | solution.py:45
  47.4 7.6 %weight_grads.2 = (f32[2048,2048]{1,0:T(8,128)}, f32[2048,2048]{1,0:T(8,128)}) custom-call(bf16[64,1024]{1,0:T(8,128)(2,1)S(1)} %get-tuple-element.62.own.refs_0_, bf16[64,1024]{1,0:T(8,128)(2,1)S(1)} %collective-permute-done.11.other.refs_1_, bf16[64,2048]{1,0:T(8,128)(2,1)S(1)} %get-tuple-element.57.scaled.refs_2_, ...), custom_call_target="tpu_custom_call" | custom-call | flops 1073741824 | bytes 25165824 | tf_op jit(solution)/shard_map/weight_grads/pallas_call | solution.py:438
  55.0 0.0 collective-permute-done.13
  55.0 0.1 fusion
  55.1 2.1 %collective-permute-start.16 = (bf16[16,2048]{1,0:T(8,128)(2,1)S(1)}, bf16[16,2048]{1,0:T(8,128)(2,1)S(1)}, u32[]{:S(2)}, u32[]{:S(2)}) collective-permute-start(bf16[16,2048]{1,0:T(8,128)(2,1)S(1)} %get-tuple-element.78), channel_id=1, source_target_pairs={{0,12},{4,8},{8,4},{12,0},{1,13},{5,9},{9,5},{13,1},{2,14},{6,10},... | collective-permute-start | bytes 196616 | tf_op jit(solution)/shard_map/ppermute | solution.py:45
  57.2 0.0 collective-permute-start.15
  57.2 2.4 %collective-permute-start.14 = (bf16[16,2048]{1,0:T(8,128)(2,1)S(1)}, bf16[16,2048]{1,0:T(8,128)(2,1)S(1)}, u32[]{:S(2)}, u32[]{:S(2)}) collective-permute-start(bf16[16,2048]{1,0:T(8,128)(2,1)S(1)} %get-tuple-element.80), channel_id=1, source_target_pairs={{0,4},{4,0},{8,12},{12,8},{1,5},{5,1},{9,13},{13,9},{2,6},{6,2},{1... | collective-permute-start | bytes 196616 | tf_op jit(solution)/shard_map/ppermute | solution.py:45
  59.5 5.1 %weight_grads.3 = f32[2048,2048]{1,0:T(8,128)} custom-call(bf16[64,2048]{1,0:T(8,128)(2,1)S(1)} %get-tuple-element.67.refs_3_.refs_0_, bf16[64,1024]{1,0:T(8,128)(2,1)S(1)} %multiply_convert_fusion.own.refs_4_.refs_1_, bf16[64,1024]{1,0:T(8,128)(2,1)S(1)} %collective-permute-done.12.other.refs_5_.refs_2_, ...), custom_call_target="tpu_custom_call", output_to_operand_aliasing={{}: (3, {})} | custom-call | flops 536870912 | bytes 12582912 | tf_op jit(solution)/shard_map/weight_grads/pallas_call | solution.py:438
  64.6 0.0 collective-permute-done.16.refs_3_
  64.7 0.0 collective-permute-done.14.refs_1_
  64.7 0.9 %final.1 = (bf16[8,2048]{1,0:T(8,128)(2,1)}, bf16[32,2048]{1,0:T(8,128)(2,1)}) custom-call(bf16[16,2048]{1,0:T(8,128)(2,1)S(1)} %get-tuple-element.81.refs_0_, bf16[16,2048]{1,0:T(8,128)(2,1)S(1)} %collective-permute-done.14.refs_1_, bf16[16,2048]{1,0:T(8,128)(2,1)S(1)} %collective-permute-done.15.refs_2_, ...), custom_call_target="tpu_custom_call" | custom-call | tf_op jit(solution)/shard_map/final/pallas_call | solution.py:472
  (8 shorter events, 0.1 us)
Async XLA Ops:
  1.8 9.4 %collective-permute-start = (bf16[16,2176]{1,0:T(8,128)(2,1)S(1)}, bf16[16,2176]{1,0:T(8,128)(2,1)S(1)}, u32[]{:S(2)}, u32[]{:S(2)}) collective-permute-start(bf16[16,2176]{1,0:T(8,128)(2,1)S(1)} %get-tuple-element.41.refs_0_), channel_id=1, source_target_pairs={{0,4},{4,0},{8,12},{12,8},{1,5},{5,1},{9,13},{13,9},{2,6},{6,2},{1... | collective-permute-start | bytes 208904 | tf_op jit(solution)/shard_map/ppermute | solution.py:45
  4.9 7.0 %collective-permute-start.2 = (bf16[16,2176]{1,0:T(8,128)(2,1)S(1)}, bf16[16,2176]{1,0:T(8,128)(2,1)S(1)}, u32[]{:S(2)}, u32[]{:S(2)}) collective-permute-start(bf16[16,2176]{1,0:T(8,128)(2,1)S(1)} %get-tuple-element.41.refs_0_), channel_id=1, source_target_pairs={{0,12},{4,8},{8,4},{12,0},{1,13},{5,9},{9,5},{13,1},{2,14},{6,10},... | collective-permute-start | bytes 208904 | tf_op jit(solution)/shard_map/ppermute | solution.py:45
  7.4 6.8 %collective-permute-start.1 = (bf16[16,2176]{1,0:T(8,128)(2,1)S(1)}, bf16[16,2176]{1,0:T(8,128)(2,1)S(1)}, u32[]{:S(2)}, u32[]{:S(2)}) collective-permute-start(bf16[16,2176]{1,0:T(8,128)(2,1)S(1)} %get-tuple-element.41.refs_0_), channel_id=1, source_target_pairs={{0,8},{4,12},{8,0},{12,4},{1,9},{5,13},{9,1},{13,5},{2,10},{6,14},... | collective-permute-start | bytes 208904 | tf_op jit(solution)/shard_map/ppermute | solution.py:45
  7.5 13.7 %collective-permute-start.3 = (bf16[16,2176]{1,0:T(8,128)(2,1)S(1)}, bf16[16,2176]{1,0:T(8,128)(2,1)S(1)}, u32[]{:S(2)}, u32[]{:S(2)}) collective-permute-start(bf16[16,2176]{1,0:T(8,128)(2,1)S(1)} %get-tuple-element.41.refs_0_), channel_id=1, source_target_pairs={{0,16},{16,0},{1,17},{17,1},{2,18},{18,2},{3,19},{19,3},{4,20},{20... | collective-permute-start | bytes 208904 | tf_op jit(solution)/shard_map/ppermute | solution.py:45
  14.1 7.0 %collective-permute-start.5 = (bf16[16,2176]{1,0:T(8,128)(2,1)S(1)}, bf16[16,2176]{1,0:T(8,128)(2,1)S(1)}, u32[]{:S(2)}, u32[]{:S(2)}) collective-permute-start(bf16[16,2176]{1,0:T(8,128)(2,1)S(1)} %collective-permute-done.1.refs_2_), channel_id=1, source_target_pairs={{0,16},{16,0},{1,17},{17,1},{2,18},{18,2},{3,19},{19,3},{4,20},{20... | collective-permute-start | bytes 208904 | tf_op jit(solution)/shard_map/ppermute | solution.py:45
  15.7 5.5 %collective-permute-start.6 = (bf16[16,2176]{1,0:T(8,128)(2,1)S(1)}, bf16[16,2176]{1,0:T(8,128)(2,1)S(1)}, u32[]{:S(2)}, u32[]{:S(2)}) collective-permute-start(bf16[16,2176]{1,0:T(8,128)(2,1)S(1)} %collective-permute-done.2.refs_3_), channel_id=1, source_target_pairs={{0,16},{16,0},{1,17},{17,1},{2,18},{18,2},{3,19},{19,3},{4,20},{20... | collective-permute-start | bytes 208904 | tf_op jit(solution)/shard_map/ppermute | solution.py:45
  16.2 5.3 %collective-permute-start.4 = (bf16[16,2176]{1,0:T(8,128)(2,1)S(1)}, bf16[16,2176]{1,0:T(8,128)(2,1)S(1)}, u32[]{:S(2)}, u32[]{:S(2)}) collective-permute-start(bf16[16,2176]{1,0:T(8,128)(2,1)S(1)} %collective-permute-done.refs_1_), channel_id=1, source_target_pairs={{0,16},{16,0},{1,17},{17,1},{2,18},{18,2},{3,19},{19,3},{4,20},{20... | collective-permute-start | bytes 208904 | tf_op jit(solution)/shard_map/ppermute | solution.py:45
  24.4 4.4 %collective-permute-start.7 = (bf16[64,1024]{1,0:T(8,128)(2,1)S(1)}, bf16[64,1024]{1,0:T(8,128)(2,1)S(1)}, u32[]{:S(2)}, u32[]{:S(2)}) collective-permute-start(bf16[64,1024]{1,0:T(8,128)(2,1)S(1)} %get-tuple-element.55), channel_id=1, source_target_pairs={{0,1},{1,0},{2,3},{3,2},{4,5},{5,4},{6,7},{7,6},{8,9},{9,8},{10,11... | collective-permute-start | bytes 393224 | tf_op jit(solution)/shard_map/ppermute | solution.py:45
  28.2 4.0 %collective-permute-start.8 = (bf16[64,1024]{1,0:T(8,128)(2,1)S(1)}, bf16[64,1024]{1,0:T(8,128)(2,1)S(1)}, u32[]{:S(2)}, u32[]{:S(2)}) collective-permute-start(bf16[64,1024]{1,0:T(8,128)(2,1)S(1)} %act_grad.3), channel_id=1, source_target_pairs={{0,1},{1,0},{2,3},{3,2},{4,5},{5,4},{6,7},{7,6},{8,9},{9,8},{10,11... | collective-permute-start | bytes 393224 | tf_op jit(solution)/shard_map/ppermute | solution.py:45
  28.8 5.5 %collective-permute-start.10 = (bf16[64,1024]{1,0:T(8,128)(2,1)S(1)}, bf16[64,1024]{1,0:T(8,128)(2,1)S(1)}, u32[]{:S(2)}, u32[]{:S(2)}) collective-permute-start(bf16[64,1024]{1,0:T(8,128)(2,1)S(1)} %fusion.1), channel_id=1, source_target_pairs={{0,2},{1,3},{2,0},{3,1},{4,6},{5,7},{6,4},{7,5},{8,10},{9,11},{10,... | collective-permute-start | bytes 393224 | tf_op jit(solution)/shard_map/ppermute | solution.py:45
  32.2 5.2 %collective-permute-start.9 = (bf16[64,1024]{1,0:T(8,128)(2,1)S(1)}, bf16[64,1024]{1,0:T(8,128)(2,1)S(1)}, u32[]{:S(2)}, u32[]{:S(2)}) collective-permute-start(bf16[64,1024]{1,0:T(8,128)(2,1)S(1)} %fusion.2), channel_id=1, source_target_pairs={{0,2},{1,3},{2,0},{3,1},{4,6},{5,7},{6,4},{7,5},{8,10},{9,11},{10,... | collective-permute-start | bytes 393224 | tf_op jit(solution)/shard_map/ppermute | solution.py:45
  34.4 3.1 %collective-permute-start.11 = (bf16[64,1024]{1,0:T(8,128)(2,1)S(1)}, bf16[64,1024]{1,0:T(8,128)(2,1)S(1)}, u32[]{:S(2)}, u32[]{:S(2)}) collective-permute-start(bf16[64,1024]{1,0:T(8,128)(2,1)S(1)} %get-tuple-element.62.own.refs_0_), channel_id=1, source_target_pairs={{0,1},{1,0},{2,3},{3,2},{4,5},{5,4},{6,7},{7,6},{8,9},{9,8},{10,11... | collective-permute-start | bytes 393224 | tf_op jit(solution)/shard_map/ppermute | solution.py:45
  39.2 3.1 %collective-permute-start.12 = (bf16[64,1024]{1,0:T(8,128)(2,1)S(1)}, bf16[64,1024]{1,0:T(8,128)(2,1)S(1)}, u32[]{:S(2)}, u32[]{:S(2)}) collective-permute-start(bf16[64,1024]{1,0:T(8,128)(2,1)S(1)} %multiply_convert_fusion.own.refs_4_.refs_1_), channel_id=1, source_target_pairs={{0,1},{1,0},{2,3},{3,2},{4,5},{5,4},{6,7},{7,6},{8,9},{9,8},{10,11... | collective-permute-start | bytes 393224 | tf_op jit(solution)/shard_map/ppermute | solution.py:45
  46.1 8.9 %collective-permute-start.13 = (bf16[4,16,2048]{2,1,0:T(8,128)(2,1)S(1)}, bf16[4,16,2048]{2,1,0:T(8,128)(2,1)S(1)}, u32[]{:S(2)}, u32[]{:S(2)}) collective-permute-start(bf16[4,16,2048]{2,1,0:T(8,128)(2,1)S(1)} %dynamic-slice_bitcast_fusion), channel_id=1, source_target_pairs={{0,16},{16,0},{1,17},{17,1},{2,18},{18,2},{3,19},{19,3},{4,20},{20... | collective-permute-start | bytes 786440 | tf_op jit(solution)/shard_map/ppermute | solution.py:45
  55.1 9.5 %collective-permute-start.16 = (bf16[16,2048]{1,0:T(8,128)(2,1)S(1)}, bf16[16,2048]{1,0:T(8,128)(2,1)S(1)}, u32[]{:S(2)}, u32[]{:S(2)}) collective-permute-start(bf16[16,2048]{1,0:T(8,128)(2,1)S(1)} %get-tuple-element.78), channel_id=1, source_target_pairs={{0,12},{4,8},{8,4},{12,0},{1,13},{5,9},{9,5},{13,1},{2,14},{6,10},... | collective-permute-start | bytes 196616 | tf_op jit(solution)/shard_map/ppermute | solution.py:45
  57.2 7.5 %collective-permute-start.15 = (bf16[16,2048]{1,0:T(8,128)(2,1)S(1)}, bf16[16,2048]{1,0:T(8,128)(2,1)S(1)}, u32[]{:S(2)}, u32[]{:S(2)}) collective-permute-start(bf16[16,2048]{1,0:T(8,128)(2,1)S(1)} %get-tuple-element.79), channel_id=1, source_target_pairs={{0,8},{4,12},{8,0},{12,4},{1,9},{5,13},{9,1},{13,5},{2,10},{6,14},... | collective-permute-start | bytes 196616 | tf_op jit(solution)/shard_map/ppermute | solution.py:45
  57.2 7.5 %collective-permute-start.14 = (bf16[16,2048]{1,0:T(8,128)(2,1)S(1)}, bf16[16,2048]{1,0:T(8,128)(2,1)S(1)}, u32[]{:S(2)}, u32[]{:S(2)}) collective-permute-start(bf16[16,2048]{1,0:T(8,128)(2,1)S(1)} %get-tuple-element.80), channel_id=1, source_target_pairs={{0,4},{4,0},{8,12},{12,8},{1,5},{5,1},{9,13},{13,9},{2,6},{6,2},{1... | collective-permute-start | bytes 196616 | tf_op jit(solution)/shard_map/ppermute | solution.py:45
